TPU v7x, 32 devices: a whole 2x2x4 slice. The times are simulated.
32 devices in a mesh: runs: 2 (over y), shot: 4 (over x, core), slab: 4 (over z).
Axes of the slice: x: 2, y: 2, z: 4, core: 2. Of those that a mesh axis runs over, the one named last changes fastest.
Arguments:
- source_now: float32 [16, 64, 16, 256], P(('runs', 'shot'), 'slab'), parts along dimension 0, may hold values from -4 to 4
- source_prev: float32 [16, 64, 16, 256], P(('runs', 'shot'), 'slab'), parts along dimension 0, may hold values from -4 to 4
- receiver_now: float32 [16, 64, 16, 256], P(('runs', 'shot'), 'slab'), parts along dimension 0, may hold values from -4 to 4
- receiver_prev: float32 [16, 64, 16, 256], P(('runs', 'shot'), 'slab'), parts along dimension 0, may hold values from -4 to 4
- courant_sq: float32 [128, 16, 256], P(('runs', 'slab')), parts along dimension 0, may hold values from 0.26 to 0.52
- source_cell: int32 [16], P(('runs', 'shot')), parts along dimension 0, may hold values from 0 to 1023
- wavelet: float32 [8, 16], P(None, ('runs', 'shot')), parts along dimension 1, may hold values from -12 to 12
- receiver_cell: int32 [16, 256], P(('runs', 'shot')), parts along dimension 0, may hold values from 0 to 1023
- traces: float32 [8, 16, 256], P(None, ('runs', 'shot')), parts along dimension 1, may hold values from -10 to 10
- offset_perm: int32 [16], P('runs'), parts along dimension 0, may hold values from 0 to 7, each once
Outputs:
- offset_image: float32 [16, 64, 16, 256], P(('runs', 'shot'), 'slab'), parts along dimension 0
- source_final: float32 [16, 64, 16, 256], P(('runs', 'shot'), 'slab'), parts along dimension 0
- receiver_final: float32 [16, 64, 16, 256], P(('runs', 'shot'), 'slab'), parts along dimension 0
There are 2 independent parts, one for each index of `runs`. A program takes and returns all parts, laid end to end along the dimension named above; each array names one. Nothing has to cross between parts.
Inputs may be any that keep to these rules, and one draw needn't show every extreme that they name: `source_cell`: a surface cell index. `receiver_cell`: surface cell indices; two receivers may share a cell. `offset_perm`: every offset index appears once.
All inputs are finite; a program needn't handle non-finite values.
Results may differ from a plain program's by a relative error of at most 0.0003.
Values sent between devices are 32-bit elements; how exact they have to be, the bound alone decides.
No kernel may reach another device: no remote copies, remote signals or barrier semaphores. Data moves between devices by JAX's collectives and lax.ppermute only.
A program may use at most 64 MiB of HBM per device.

v0:
```python
import jax
import jax.numpy as jnp
from jax import lax
from jax.sharding import PartitionSpec as P

OFF_DEV = 2
STEPS = 8
INJECT_Z = 4
stencil_weights = (-205.0 / 72.0, 8.0 / 5.0, -1.0 / 5.0, 8.0 / 315.0, -1.0 / 560.0)
side_weight = 1.0 / 16.0


def extended_2(cells, sides, width):
    for axis, dim in sides:
        count = lax.axis_size(axis)
        ends = count - 1
        head = lax.slice_in_dim(cells, 0, width, axis=dim)
        tail = lax.slice_in_dim(cells, cells.shape[dim] - width, cells.shape[dim], axis=dim)
        cells = jnp.concatenate(
            [
                lax.ppermute(tail, axis, [(i, (i + 1) % count) for i in range(ends)]),
                cells,
                lax.ppermute(head, axis, [((i + 1) % count, i) for i in range(ends)]),
            ],
            axis=dim,
        )
    return cells


def laplace_rows(extended):
    row_count = extended.shape[2] - 8
    centre = extended[:, :, 4 : 4 + row_count]
    size_y = centre.shape[3]
    size_z = centre.shape[4]
    padded = jnp.pad(centre, ((0, 0), (0, 0), (0, 0), (4, 4), (4, 4)))
    summed = (1.0 + 2.0 * side_weight) * stencil_weights[0] * centre
    for distance in range(1, 5):
        weight = stencil_weights[distance]
        summed = summed + weight * (
            extended[:, :, 4 + distance : 4 + distance + row_count]
            + extended[:, :, 4 - distance : 4 - distance + row_count]
        )
        summed = summed + side_weight * weight * (
            padded[:, :, :, 4 + distance : 4 + distance + size_y, 4 : 4 + size_z]
            + padded[:, :, :, 4 - distance : 4 - distance + size_y, 4 : 4 + size_z]
        )
        summed = summed + side_weight * weight * (
            padded[:, :, :, 4 : 4 + size_y, 4 + distance : 4 + distance + size_z]
            + padded[:, :, :, 4 : 4 + size_y, 4 - distance : 4 - distance + size_z]
        )
    return summed


def hot_tables(source_cell, receiver_cell, first_row, row_count, cells_y):
    positions = lax.broadcasted_iota(jnp.int32, (1, row_count * cells_y), 1) + first_row * cells_y
    source_hot = (source_cell[:, None] == positions).astype(jnp.float32)
    receiver_hot = (receiver_cell[:, :, None] == positions[None]).astype(jnp.float32)
    return (source_hot, receiver_hot)


def correlate(source_pad, receiver_pad, shift_by, half_span, extent):
    shifted_source = lax.dynamic_slice_in_dim(source_pad, half_span - shift_by, extent, axis=2)
    shifted_receiver = lax.dynamic_slice_in_dim(receiver_pad, half_span + shift_by, extent, axis=2)
    return jnp.sum(shifted_source * shifted_receiver, axis=0)


def body(
    source_now,
    source_prev,
    receiver_now,
    receiver_prev,
    courant_sq,
    source_cell,
    wavelet,
    receiver_cell,
    traces,
    offset_perm,
):
    shots_here, rows_here, cells_y, cells_z = source_now.shape
    slab_start = lax.axis_index("slab") * rows_here
    grid_rows = rows_here * lax.axis_size("slab")
    fields = jnp.stack([source_now, receiver_now])
    before = jnp.stack([source_prev, receiver_prev])
    local_tables = hot_tables(source_cell, receiver_cell, slab_start, rows_here, cells_y)
    for moment in range(STEPS):
        extended = extended_2(fields, (("slab", 2),), 4)
        row_count = extended.shape[2] - 8
        centre = extended[:, :, 4 : 4 + row_count]
        updated = 2.0 * centre - before + courant_sq * laplace_rows(extended)
        source_hot, receiver_hot = local_tables
        source_plane = source_hot * wavelet[moment][:, None]
        receiver_plane = jnp.einsum(
            "sr,src->sc", traces[moment], receiver_hot, precision=lax.Precision.HIGHEST
        )
        planes = jnp.stack([source_plane, receiver_plane]).reshape(
            2, shots_here, row_count, cells_y
        )
        updated = updated.at[:, :, :, :, INJECT_Z].add(planes)
        global_rows = slab_start + lax.broadcasted_iota(jnp.int32, (row_count,), 0)
        inside = (global_rows >= 0) & (global_rows < grid_rows)
        updated = jnp.where(inside[None, None, :, None, None], updated, 0.0)
        before, fields = (fields, updated)
    half_span = offset_perm.shape[0] // 2
    pad_widths = ((0, 0), (0, 0), (half_span, half_span), (0, 0))
    own_lags = lax.dynamic_slice_in_dim(offset_perm, lax.axis_index("shot") * OFF_DEV, OFF_DEV)
    shard_piece = lax.all_gather(fields, "shot", axis=1, tiled=True)
    source_pad = jnp.pad(shard_piece[0], pad_widths)
    receiver_pad = jnp.pad(shard_piece[1], pad_widths)
    products = [
        correlate(source_pad, receiver_pad, own_lags[slot_index] - half_span, half_span, cells_y)
        for slot_index in range(OFF_DEV)
    ]
    offset_image = jnp.stack(products)
    return (offset_image, fields[0], fields[1])


def solution(mesh):
    in_specs = (
        P(("runs", "shot"), "slab", None, None),
        P(("runs", "shot"), "slab", None, None),
        P(("runs", "shot"), "slab", None, None),
        P(("runs", "shot"), "slab", None, None),
        P(("runs", "slab"), None, None),
        P(("runs", "shot")),
        P(None, ("runs", "shot")),
        P(("runs", "shot"), None),
        P(None, ("runs", "shot"), None),
        P("runs"),
    )
    out_specs = (
        P(("runs", "shot"), "slab", None, None),
        P(("runs", "shot"), "slab", None, None),
        P(("runs", "shot"), "slab", None, None),
    )
    return jax.shard_map(body, mesh=mesh, in_specs=in_specs, out_specs=out_specs, check_vma=False)
```

profile of v0, /device:TPU:0, one launch (start us, length us, event | category | flops | bytes accessed | tf_op | source)
XLA Modules:
  0.0 271.8 jit_solution(146948616227826346)
XLA Ops:
  9.9 5.6 %collective-permute-start.1 = (f32[2,2,4,16,256]{4,3,2,1,0:T(8,128)S(1)}, f32[2,2,4,16,256]{4,3,2,1,0:T(8,128)S(1)}, u32[]{:S(2)}, u32[]{:S(2)}) collective-permute-start(f32[2,2,4,16,256]{4,3,2,1,0:T(8,128)S(1)} %get-tuple-element.139), channel_id=1, source_target_pairs={{0,1},{1,2},{2,3},{4,5},{5,6},{6,7},{8,9},{9,10},{10,11},{12,13},{... | collective-permute-start | bytes 786440 | tf_op jit(solution)/shard_map/ppermute | solution.py:21
  25.1 5.3 %scatter-add.26 = f32[2,2,16,16,256]{4,3,2,1,0:T(8,128)S(1)} dynamic-update-slice(f32[2,2,16,16,256]{4,3,2,1,0:T(8,128)S(1)} %fusion.216, f32[2,2,16,16,1]{4,3,2,1,0:T(8,128)S(1)} %copy.241, s32[]{:T(128)} %constant.214.clone.1, s32[]{:T(128)} %constant.214.clone.1, s32[]{:T(128)} %constant.214.clone.1, s32[]{:T(128)} %constant.214.clone.1, s32[]{:T(128)} %constant.228.clone.1) | dynamic-update-slice | bytes 8196 | tf_op jit(solution)/shard_map/scatter-add | solution.py:98
  33.0 5.7 %collective-permute-start.3 = (f32[2,2,4,16,256]{4,3,2,1,0:T(8,128)S(1)}, f32[2,2,4,16,256]{4,3,2,1,0:T(8,128)}, u32[]{:S(2)}, u32[]{:S(2)}) collective-permute-start(f32[2,2,4,16,256]{4,3,2,1,0:T(8,128)S(1)} %get-tuple-element.135), channel_id=1, source_target_pairs={{0,1},{1,2},{2,3},{4,5},{5,6},{6,7},{8,9},{9,10},{10,11},{12,13},{... | collective-permute-start | bytes 786440 | tf_op jit(solution)/shard_map/ppermute | solution.py:21
  42.7 14.2 %fusion.186 = f32[2,2,16,16,256]{4,3,2,1,0:T(8,128)S(1)} fusion(f32[2,2,16,16,256]{4,3,2,1,0:T(8,128)} %copy-done.10, f32[2,2,4,16,256]{4,3,2,1,0:T(8,128)} %collective-permute-done.3, f32[2,2,4,16,256]{4,3,2,1,0:T(8,128)} %copy-done.13, f32[16,16,256]{2,1,0:T(8,128)S(1)} %copy-done, f32[1,2,16,16,256]{4,3,2,1,0:T(8,128)S(1)} %bitcast.77, ...), kind=kLoop, calls=%fused_computation.411 | loop fusion | flops 13107200 | bytes 3932160 | tf_op jit(solution)/shard_map/add | solution.py:89
  58.0 6.7 %scatter-add.29 = f32[2,2,16,16,256]{4,3,2,1,0:T(8,128)} dynamic-update-slice(f32[2,2,16,16,256]{4,3,2,1,0:T(8,128)} %copy-done.5, f32[2,2,16,16,1]{4,3,2,1,0:T(8,128)S(1)} %copy.244, s32[]{:T(128)} %constant.214.clone.1, s32[]{:T(128)} %constant.214.clone.1, s32[]{:T(128)} %constant.214.clone.1, s32[]{:T(128)} %constant.214.clone.1, s32[]{:T(128)} %constant.228.clone.1) | dynamic-update-slice | bytes 8196 | tf_op jit(solution)/shard_map/scatter-add | solution.py:98
  67.5 5.1 %collective-permute-start.5 = (f32[2,2,4,16,256]{4,3,2,1,0:T(8,128)S(1)}, f32[2,2,4,16,256]{4,3,2,1,0:T(8,128)S(1)}, u32[]{:S(2)}, u32[]{:S(2)}) collective-permute-start(f32[2,2,4,16,256]{4,3,2,1,0:T(8,128)S(1)} %get-tuple-element.133), channel_id=1, source_target_pairs={{0,1},{1,2},{2,3},{4,5},{5,6},{6,7},{8,9},{9,10},{10,11},{12,13},{... | collective-permute-start | bytes 786440 | tf_op jit(solution)/shard_map/ppermute | solution.py:21
  76.5 4.5 %fusion.160 = f32[2,2,16,16,256]{4,3,2,1,0:T(8,128)} fusion(f32[2,2,16,16,256]{4,3,2,1,0:T(8,128)S(1)} %broadcast_select_fusion.6, f32[2,2,4,16,256]{4,3,2,1,0:T(8,128)S(1)} %collective-permute-done.5, f32[2,2,4,16,256]{4,3,2,1,0:T(8,128)S(1)} %collective-permute-done.4, f32[16,16,256]{2,1,0:T(8,128)S(1)} %copy-done, ...), kind=kLoop, calls=%fused_computation.385 | loop fusion | flops 13107200 | bytes 3932176 | tf_op jit(solution)/shard_map/add | solution.py:89
  83.1 6.7 %scatter-add.30 = f32[2,2,16,16,256]{4,3,2,1,0:T(8,128)} dynamic-update-slice(f32[2,2,16,16,256]{4,3,2,1,0:T(8,128)} %fusion.160, f32[2,2,16,16,1]{4,3,2,1,0:T(8,128)S(1)} %copy.247, s32[]{:T(128)} %constant.214.clone.1, s32[]{:T(128)} %constant.214.clone.1, s32[]{:T(128)} %constant.214.clone.1, s32[]{:T(128)} %constant.214.clone.1, s32[]{:T(128)} %constant.228.clone.1) | dynamic-update-slice | bytes 8196 | tf_op jit(solution)/shard_map/scatter-add | solution.py:98
  92.7 5.2 %collective-permute-start.7 = (f32[2,2,4,16,256]{4,3,2,1,0:T(8,128)S(1)}, f32[2,2,4,16,256]{4,3,2,1,0:T(8,128)S(1)}, u32[]{:S(2)}, u32[]{:S(2)}) collective-permute-start(f32[2,2,4,16,256]{4,3,2,1,0:T(8,128)S(1)} %get-tuple-element.131), channel_id=1, source_target_pairs={{0,1},{1,2},{2,3},{4,5},{5,6},{6,7},{8,9},{9,10},{10,11},{12,13},{... | collective-permute-start | bytes 786440 | tf_op jit(solution)/shard_map/ppermute | solution.py:21
  101.5 4.5 %fusion.134 = f32[2,2,16,16,256]{4,3,2,1,0:T(8,128)} fusion(f32[2,2,16,16,256]{4,3,2,1,0:T(8,128)S(1)} %broadcast_select_fusion.5, f32[2,2,4,16,256]{4,3,2,1,0:T(8,128)S(1)} %collective-permute-done.7, f32[2,2,4,16,256]{4,3,2,1,0:T(8,128)S(1)} %collective-permute-done.6, f32[16,16,256]{2,1,0:T(8,128)S(1)} %copy-done, ...), kind=kLoop, calls=%fused_computation.359 | loop fusion | flops 13107200 | bytes 3932176 | tf_op jit(solution)/shard_map/add | solution.py:89
  108.2 6.7 %scatter-add.31 = f32[2,2,16,16,256]{4,3,2,1,0:T(8,128)} dynamic-update-slice(f32[2,2,16,16,256]{4,3,2,1,0:T(8,128)} %fusion.134, f32[2,2,16,16,1]{4,3,2,1,0:T(8,128)S(1)} %copy.250, s32[]{:T(128)} %constant.214.clone.1, s32[]{:T(128)} %constant.214.clone.1, s32[]{:T(128)} %constant.214.clone.1, s32[]{:T(128)} %constant.214.clone.1, s32[]{:T(128)} %constant.228.clone.1) | dynamic-update-slice | bytes 8196 | tf_op jit(solution)/shard_map/scatter-add | solution.py:98
  117.7 5.0 %collective-permute-start.9 = (f32[2,2,4,16,256]{4,3,2,1,0:T(8,128)S(1)}, f32[2,2,4,16,256]{4,3,2,1,0:T(8,128)S(1)}, u32[]{:S(2)}, u32[]{:S(2)}) collective-permute-start(f32[2,2,4,16,256]{4,3,2,1,0:T(8,128)S(1)} %get-tuple-element.129), channel_id=1, source_target_pairs={{0,1},{1,2},{2,3},{4,5},{5,6},{6,7},{8,9},{9,10},{10,11},{12,13},{... | collective-permute-start | bytes 786440 | tf_op jit(solution)/shard_map/ppermute | solution.py:21
  126.6 4.5 %fusion.108 = f32[2,2,16,16,256]{4,3,2,1,0:T(8,128)} fusion(f32[2,2,16,16,256]{4,3,2,1,0:T(8,128)S(1)} %broadcast_select_fusion.4, f32[2,2,4,16,256]{4,3,2,1,0:T(8,128)S(1)} %collective-permute-done.9, f32[2,2,4,16,256]{4,3,2,1,0:T(8,128)S(1)} %collective-permute-done.8, f32[16,16,256]{2,1,0:T(8,128)S(1)} %copy-done, ...), kind=kLoop, calls=%fused_computation.333 | loop fusion | flops 13107200 | bytes 3932176 | tf_op jit(solution)/shard_map/add | solution.py:89
  133.2 6.7 %scatter-add.34 = f32[2,2,16,16,256]{4,3,2,1,0:T(8,128)} dynamic-update-slice(f32[2,2,16,16,256]{4,3,2,1,0:T(8,128)} %fusion.108, f32[2,2,16,16,1]{4,3,2,1,0:T(8,128)S(1)} %copy.253, s32[]{:T(128)} %constant.214.clone.1, s32[]{:T(128)} %constant.214.clone.1, s32[]{:T(128)} %constant.214.clone.1, s32[]{:T(128)} %constant.214.clone.1, s32[]{:T(128)} %constant.228.clone.1) | dynamic-update-slice | bytes 8196 | tf_op jit(solution)/shard_map/scatter-add | solution.py:98
  142.7 5.0 %collective-permute-start.11 = (f32[2,2,4,16,256]{4,3,2,1,0:T(8,128)S(1)}, f32[2,2,4,16,256]{4,3,2,1,0:T(8,128)S(1)}, u32[]{:S(2)}, u32[]{:S(2)}) collective-permute-start(f32[2,2,4,16,256]{4,3,2,1,0:T(8,128)S(1)} %get-tuple-element.127), channel_id=1, source_target_pairs={{0,1},{1,2},{2,3},{4,5},{5,6},{6,7},{8,9},{9,10},{10,11},{12,13},{... | collective-permute-start | bytes 786440 | tf_op jit(solution)/shard_map/ppermute | solution.py:21
  151.6 4.5 %fusion.82 = f32[2,2,16,16,256]{4,3,2,1,0:T(8,128)} fusion(f32[2,2,16,16,256]{4,3,2,1,0:T(8,128)S(1)} %broadcast_select_fusion.3, f32[2,2,4,16,256]{4,3,2,1,0:T(8,128)S(1)} %collective-permute-done.11, f32[2,2,4,16,256]{4,3,2,1,0:T(8,128)S(1)} %collective-permute-done.10, f32[16,16,256]{2,1,0:T(8,128)S(1)} %copy-done, ...), kind=kLoop, calls=%fused_computation.307 | loop fusion | flops 13107200 | bytes 3932176 | tf_op jit(solution)/shard_map/add | solution.py:89
  158.3 6.7 %scatter-add.35 = f32[2,2,16,16,256]{4,3,2,1,0:T(8,128)} dynamic-update-slice(f32[2,2,16,16,256]{4,3,2,1,0:T(8,128)} %fusion.82, f32[2,2,16,16,1]{4,3,2,1,0:T(8,128)S(1)} %copy.256, s32[]{:T(128)} %constant.214.clone.1, s32[]{:T(128)} %constant.214.clone.1, s32[]{:T(128)} %constant.214.clone.1, s32[]{:T(128)} %constant.214.clone.1, s32[]{:T(128)} %constant.228.clone.1) | dynamic-update-slice | bytes 8196 | tf_op jit(solution)/shard_map/scatter-add | solution.py:98
  167.8 5.3 %collective-permute-start.13 = (f32[2,2,4,16,256]{4,3,2,1,0:T(8,128)S(1)}, f32[2,2,4,16,256]{4,3,2,1,0:T(8,128)S(1)}, u32[]{:S(2)}, u32[]{:S(2)}) collective-permute-start(f32[2,2,4,16,256]{4,3,2,1,0:T(8,128)S(1)} %get-tuple-element.125), channel_id=1, source_target_pairs={{0,1},{1,2},{2,3},{4,5},{5,6},{6,7},{8,9},{9,10},{10,11},{12,13},{... | collective-permute-start | bytes 786440 | tf_op jit(solution)/shard_map/ppermute | solution.py:21
  176.7 4.5 %fusion.56 = f32[2,2,16,16,256]{4,3,2,1,0:T(8,128)} fusion(f32[2,2,16,16,256]{4,3,2,1,0:T(8,128)S(1)} %broadcast_select_fusion.2, f32[2,2,4,16,256]{4,3,2,1,0:T(8,128)S(1)} %collective-permute-done.13, f32[2,2,4,16,256]{4,3,2,1,0:T(8,128)S(1)} %collective-permute-done.12, f32[16,16,256]{2,1,0:T(8,128)S(1)} %copy-done, ...), kind=kLoop, calls=%fused_computation.281 | loop fusion | flops 13107200 | bytes 3932176 | tf_op jit(solution)/shard_map/add | solution.py:89
  183.3 6.7 %scatter-add.36 = f32[2,2,16,16,256]{4,3,2,1,0:T(8,128)} dynamic-update-slice(f32[2,2,16,16,256]{4,3,2,1,0:T(8,128)} %fusion.56, f32[2,2,16,16,1]{4,3,2,1,0:T(8,128)S(1)} %copy.259, s32[]{:T(128)} %constant.214.clone.1, s32[]{:T(128)} %constant.214.clone.1, s32[]{:T(128)} %constant.214.clone.1, s32[]{:T(128)} %constant.214.clone.1, s32[]{:T(128)} %constant.228.clone.1) | dynamic-update-slice | bytes 8196 | tf_op jit(solution)/shard_map/scatter-add | solution.py:98
  192.8 5.0 %collective-permute-start.15 = (f32[2,2,4,16,256]{4,3,2,1,0:T(8,128)S(1)}, f32[2,2,4,16,256]{4,3,2,1,0:T(8,128)S(1)}, u32[]{:S(2)}, u32[]{:S(2)}) collective-permute-start(f32[2,2,4,16,256]{4,3,2,1,0:T(8,128)S(1)} %get-tuple-element.123), channel_id=1, source_target_pairs={{0,1},{1,2},{2,3},{4,5},{5,6},{6,7},{8,9},{9,10},{10,11},{12,13},{... | collective-permute-start | bytes 786440 | tf_op jit(solution)/shard_map/ppermute | solution.py:21
  201.7 4.5 %fusion.30 = f32[2,2,16,16,256]{4,3,2,1,0:T(8,128)} fusion(f32[2,2,16,16,256]{4,3,2,1,0:T(8,128)S(1)} %broadcast_select_fusion.1, f32[2,2,4,16,256]{4,3,2,1,0:T(8,128)S(1)} %collective-permute-done.15, f32[2,2,4,16,256]{4,3,2,1,0:T(8,128)S(1)} %collective-permute-done.14, f32[16,16,256]{2,1,0:T(8,128)S(1)} %copy-done, ...), kind=kLoop, calls=%fused_computation.255 | loop fusion | flops 13107200 | bytes 3932176 | tf_op jit(solution)/shard_map/add | solution.py:89
  208.4 6.7 %scatter-add.39 = f32[2,2,16,16,256]{4,3,2,1,0:T(8,128)} dynamic-update-slice(f32[2,2,16,16,256]{4,3,2,1,0:T(8,128)} %fusion.30, f32[2,2,16,16,1]{4,3,2,1,0:T(8,128)S(1)} %copy.262, s32[]{:T(128)} %constant.214.clone.1, s32[]{:T(128)} %constant.214.clone.1, s32[]{:T(128)} %constant.214.clone.1, s32[]{:T(128)} %constant.214.clone.1, s32[]{:T(128)} %constant.228.clone.1) | dynamic-update-slice | bytes 8196 | tf_op jit(solution)/shard_map/scatter-add | solution.py:98
  224.5 30.6 %all-gather.2.cloned.1.call-done = f32[2,8,16,16,256]{4,3,2,1,0:T(8,128)} async-done(((f32[2,2,16,16,256]{4,3,2,1,0:T(8,128)}), f32[2,8,16,16,256]{4,3,2,1,0:T(8,128)}) %all-gather.2.cloned.1.call-update) | async-done | bytes 4194320 | tf_op jit(solution)/shard_map/all_gather | solution.py:106
  (175 shorter events, 85.8 us)
Async XLA Ops:
  7.2 8.4 %copy-start.9 = (f32[2,16,16,256]{3,2,1,0:T(8,128)S(1)}, f32[2,16,16,256]{3,2,1,0:T(8,128)}, u32[]{:S(2)}) copy-start(f32[2,16,16,256]{3,2,1,0:T(8,128)} %param.26) | copy-start | bytes 1572868
  7.2 247.9 %all-gather.2.cloned.1.call-start = ((), (), s32[]{:S(2)}) async-start(), calls=%async_computation | async-start | bytes 5242880 | tf_op jit(solution)/shard_map/all_gather | solution.py:106
  8.5 9.2 %copy-start.21 = (s32[2]{0:T(128)S(1)}, s32[2]{0:T(128)}, u32[]{:S(2)}) copy-start(s32[2]{0:T(128)} %param.31) | copy-start | bytes 28
  8.5 11.4 %collective-permute-start = (f32[2,2,4,16,256]{4,3,2,1,0:T(8,128)S(1)}, f32[2,2,4,16,256]{4,3,2,1,0:T(8,128)S(1)}, u32[]{:S(2)}, u32[]{:S(2)}) collective-permute-start(f32[2,2,4,16,256]{4,3,2,1,0:T(8,128)S(1)} %get-tuple-element.138), channel_id=1, source_target_pairs={{1,0},{2,1},{3,2},{5,4},{6,5},{7,6},{9,8},{10,9},{11,10},{13,12},{... | collective-permute-start | bytes 786440 | tf_op jit(solution)/shard_map/ppermute | solution.py:23
  9.9 11.1 %collective-permute-start.1 = (f32[2,2,4,16,256]{4,3,2,1,0:T(8,128)S(1)}, f32[2,2,4,16,256]{4,3,2,1,0:T(8,128)S(1)}, u32[]{:S(2)}, u32[]{:S(2)}) collective-permute-start(f32[2,2,4,16,256]{4,3,2,1,0:T(8,128)S(1)} %get-tuple-element.139), channel_id=1, source_target_pairs={{0,1},{1,2},{2,3},{4,5},{5,6},{6,7},{8,9},{9,10},{10,11},{12,13},{... | collective-permute-start | bytes 786440 | tf_op jit(solution)/shard_map/ppermute | solution.py:21
  31.7 9.8 %collective-permute-start.2 = (f32[2,2,4,16,256]{4,3,2,1,0:T(8,128)S(1)}, f32[2,2,4,16,256]{4,3,2,1,0:T(8,128)S(1)}, u32[]{:S(2)}, u32[]{:S(2)}) collective-permute-start(f32[2,2,4,16,256]{4,3,2,1,0:T(8,128)S(1)} %get-tuple-element.134), channel_id=1, source_target_pairs={{1,0},{2,1},{3,2},{5,4},{6,5},{7,6},{9,8},{10,9},{11,10},{13,12},{... | collective-permute-start | bytes 786440 | tf_op jit(solution)/shard_map/ppermute | solution.py:23
  33.0 9.7 %collective-permute-start.3 = (f32[2,2,4,16,256]{4,3,2,1,0:T(8,128)S(1)}, f32[2,2,4,16,256]{4,3,2,1,0:T(8,128)}, u32[]{:S(2)}, u32[]{:S(2)}) collective-permute-start(f32[2,2,4,16,256]{4,3,2,1,0:T(8,128)S(1)} %get-tuple-element.135), channel_id=1, source_target_pairs={{0,1},{1,2},{2,3},{4,5},{5,6},{6,7},{8,9},{9,10},{10,11},{12,13},{... | collective-permute-start | bytes 786440 | tf_op jit(solution)/shard_map/ppermute | solution.py:21
  66.2 9.1 %collective-permute-start.4 = (f32[2,2,4,16,256]{4,3,2,1,0:T(8,128)S(1)}, f32[2,2,4,16,256]{4,3,2,1,0:T(8,128)S(1)}, u32[]{:S(2)}, u32[]{:S(2)}) collective-permute-start(f32[2,2,4,16,256]{4,3,2,1,0:T(8,128)S(1)} %get-tuple-element.132), channel_id=1, source_target_pairs={{1,0},{2,1},{3,2},{5,4},{6,5},{7,6},{9,8},{10,9},{11,10},{13,12},{... | collective-permute-start | bytes 786440 | tf_op jit(solution)/shard_map/ppermute | solution.py:23
  67.5 9.0 %collective-permute-start.5 = (f32[2,2,4,16,256]{4,3,2,1,0:T(8,128)S(1)}, f32[2,2,4,16,256]{4,3,2,1,0:T(8,128)S(1)}, u32[]{:S(2)}, u32[]{:S(2)}) collective-permute-start(f32[2,2,4,16,256]{4,3,2,1,0:T(8,128)S(1)} %get-tuple-element.133), channel_id=1, source_target_pairs={{0,1},{1,2},{2,3},{4,5},{5,6},{6,7},{8,9},{9,10},{10,11},{12,13},{... | collective-permute-start | bytes 786440 | tf_op jit(solution)/shard_map/ppermute | solution.py:21
  89.9 11.7 %copy-start.6 = (f32[2,2,16,16,256]{4,3,2,1,0:T(8,128)S(1)}, f32[2,2,16,16,256]{4,3,2,1,0:T(8,128)}, u32[]{:S(2)}) copy-start(f32[2,2,16,16,256]{4,3,2,1,0:T(8,128)} %scatter-add.29) | copy-start | bytes 3145732
  91.4 8.7 %collective-permute-start.6 = (f32[2,2,4,16,256]{4,3,2,1,0:T(8,128)S(1)}, f32[2,2,4,16,256]{4,3,2,1,0:T(8,128)S(1)}, u32[]{:S(2)}, u32[]{:S(2)}) collective-permute-start(f32[2,2,4,16,256]{4,3,2,1,0:T(8,128)S(1)} %get-tuple-element.130), channel_id=1, source_target_pairs={{1,0},{2,1},{3,2},{5,4},{6,5},{7,6},{9,8},{10,9},{11,10},{13,12},{... | collective-permute-start | bytes 786440 | tf_op jit(solution)/shard_map/ppermute | solution.py:23
  92.7 8.9 %collective-permute-start.7 = (f32[2,2,4,16,256]{4,3,2,1,0:T(8,128)S(1)}, f32[2,2,4,16,256]{4,3,2,1,0:T(8,128)S(1)}, u32[]{:S(2)}, u32[]{:S(2)}) collective-permute-start(f32[2,2,4,16,256]{4,3,2,1,0:T(8,128)S(1)} %get-tuple-element.131), channel_id=1, source_target_pairs={{0,1},{1,2},{2,3},{4,5},{5,6},{6,7},{8,9},{9,10},{10,11},{12,13},{... | collective-permute-start | bytes 786440 | tf_op jit(solution)/shard_map/ppermute | solution.py:21
  114.9 11.7 %copy-start.1 = (f32[2,2,16,16,256]{4,3,2,1,0:T(8,128)S(1)}, f32[2,2,16,16,256]{4,3,2,1,0:T(8,128)}, u32[]{:S(2)}) copy-start(f32[2,2,16,16,256]{4,3,2,1,0:T(8,128)} %scatter-add.30) | copy-start | bytes 3145732
  116.4 8.7 %collective-permute-start.8 = (f32[2,2,4,16,256]{4,3,2,1,0:T(8,128)S(1)}, f32[2,2,4,16,256]{4,3,2,1,0:T(8,128)S(1)}, u32[]{:S(2)}, u32[]{:S(2)}) collective-permute-start(f32[2,2,4,16,256]{4,3,2,1,0:T(8,128)S(1)} %get-tuple-element.128), channel_id=1, source_target_pairs={{1,0},{2,1},{3,2},{5,4},{6,5},{7,6},{9,8},{10,9},{11,10},{13,12},{... | collective-permute-start | bytes 786440 | tf_op jit(solution)/shard_map/ppermute | solution.py:23
  117.7 8.9 %collective-permute-start.9 = (f32[2,2,4,16,256]{4,3,2,1,0:T(8,128)S(1)}, f32[2,2,4,16,256]{4,3,2,1,0:T(8,128)S(1)}, u32[]{:S(2)}, u32[]{:S(2)}) collective-permute-start(f32[2,2,4,16,256]{4,3,2,1,0:T(8,128)S(1)} %get-tuple-element.129), channel_id=1, source_target_pairs={{0,1},{1,2},{2,3},{4,5},{5,6},{6,7},{8,9},{9,10},{10,11},{12,13},{... | collective-permute-start | bytes 786440 | tf_op jit(solution)/shard_map/ppermute | solution.py:21
  139.9 11.7 %copy-start.2 = (f32[2,2,16,16,256]{4,3,2,1,0:T(8,128)S(1)}, f32[2,2,16,16,256]{4,3,2,1,0:T(8,128)}, u32[]{:S(2)}) copy-start(f32[2,2,16,16,256]{4,3,2,1,0:T(8,128)} %scatter-add.31) | copy-start | bytes 3145732
  141.4 8.7 %collective-permute-start.10 = (f32[2,2,4,16,256]{4,3,2,1,0:T(8,128)S(1)}, f32[2,2,4,16,256]{4,3,2,1,0:T(8,128)S(1)}, u32[]{:S(2)}, u32[]{:S(2)}) collective-permute-start(f32[2,2,4,16,256]{4,3,2,1,0:T(8,128)S(1)} %get-tuple-element.126), channel_id=1, source_target_pairs={{1,0},{2,1},{3,2},{5,4},{6,5},{7,6},{9,8},{10,9},{11,10},{13,12},{... | collective-permute-start | bytes 786440 | tf_op jit(solution)/shard_map/ppermute | solution.py:23
  142.7 8.9 %collective-permute-start.11 = (f32[2,2,4,16,256]{4,3,2,1,0:T(8,128)S(1)}, f32[2,2,4,16,256]{4,3,2,1,0:T(8,128)S(1)}, u32[]{:S(2)}, u32[]{:S(2)}) collective-permute-start(f32[2,2,4,16,256]{4,3,2,1,0:T(8,128)S(1)} %get-tuple-element.127), channel_id=1, source_target_pairs={{0,1},{1,2},{2,3},{4,5},{5,6},{6,7},{8,9},{9,10},{10,11},{12,13},{... | collective-permute-start | bytes 786440 | tf_op jit(solution)/shard_map/ppermute | solution.py:21
  165.0 11.7 %copy-start.3 = (f32[2,2,16,16,256]{4,3,2,1,0:T(8,128)S(1)}, f32[2,2,16,16,256]{4,3,2,1,0:T(8,128)}, u32[]{:S(2)}) copy-start(f32[2,2,16,16,256]{4,3,2,1,0:T(8,128)} %scatter-add.34) | copy-start | bytes 3145732
  166.5 8.7 %collective-permute-start.12 = (f32[2,2,4,16,256]{4,3,2,1,0:T(8,128)S(1)}, f32[2,2,4,16,256]{4,3,2,1,0:T(8,128)S(1)}, u32[]{:S(2)}, u32[]{:S(2)}) collective-permute-start(f32[2,2,4,16,256]{4,3,2,1,0:T(8,128)S(1)} %get-tuple-element.124), channel_id=1, source_target_pairs={{1,0},{2,1},{3,2},{5,4},{6,5},{7,6},{9,8},{10,9},{11,10},{13,12},{... | collective-permute-start | bytes 786440 | tf_op jit(solution)/shard_map/ppermute | solution.py:23
  167.8 8.9 %collective-permute-start.13 = (f32[2,2,4,16,256]{4,3,2,1,0:T(8,128)S(1)}, f32[2,2,4,16,256]{4,3,2,1,0:T(8,128)S(1)}, u32[]{:S(2)}, u32[]{:S(2)}) collective-permute-start(f32[2,2,4,16,256]{4,3,2,1,0:T(8,128)S(1)} %get-tuple-element.125), channel_id=1, source_target_pairs={{0,1},{1,2},{2,3},{4,5},{5,6},{6,7},{8,9},{9,10},{10,11},{12,13},{... | collective-permute-start | bytes 786440 | tf_op jit(solution)/shard_map/ppermute | solution.py:21
  190.0 11.7 %copy-start.4 = (f32[2,2,16,16,256]{4,3,2,1,0:T(8,128)S(1)}, f32[2,2,16,16,256]{4,3,2,1,0:T(8,128)}, u32[]{:S(2)}) copy-start(f32[2,2,16,16,256]{4,3,2,1,0:T(8,128)} %scatter-add.35) | copy-start | bytes 3145732
  191.5 8.7 %collective-permute-start.14 = (f32[2,2,4,16,256]{4,3,2,1,0:T(8,128)S(1)}, f32[2,2,4,16,256]{4,3,2,1,0:T(8,128)S(1)}, u32[]{:S(2)}, u32[]{:S(2)}) collective-permute-start(f32[2,2,4,16,256]{4,3,2,1,0:T(8,128)S(1)} %get-tuple-element.122), channel_id=1, source_target_pairs={{1,0},{2,1},{3,2},{5,4},{6,5},{7,6},{9,8},{10,9},{11,10},{13,12},{... | collective-permute-start | bytes 786440 | tf_op jit(solution)/shard_map/ppermute | solution.py:23
  192.8 8.9 %collective-permute-start.15 = (f32[2,2,4,16,256]{4,3,2,1,0:T(8,128)S(1)}, f32[2,2,4,16,256]{4,3,2,1,0:T(8,128)S(1)}, u32[]{:S(2)}, u32[]{:S(2)}) collective-permute-start(f32[2,2,4,16,256]{4,3,2,1,0:T(8,128)S(1)} %get-tuple-element.123), channel_id=1, source_target_pairs={{0,1},{1,2},{2,3},{4,5},{5,6},{6,7},{8,9},{9,10},{10,11},{12,13},{... | collective-permute-start | bytes 786440 | tf_op jit(solution)/shard_map/ppermute | solution.py:21
  (22 other events, 120.4 us)
Sparse Core Ops, SparseCore 0:
  217.7 37.3 all-gather.1
where the time goes:
time: 273 us; the launch traced here: 272 us
  local copies, waits for them, and re-layouts  80.7 us (30%)
  other arithmetic  59.1 us (22%)
  waiting for transfers between devices  57 us (21%)
  starting transfers between devices  52.5 us (19%)
  between operations  19.9 us (7%)
    scatter-add x8, local copies, waits for them, and re-layouts, body(): updated = updated.at[:, :, :, :, INJECT_Z].add(planes)  52.5 us
    add x8, other arithmetic, body(): updated = 2.0 * centre - before + courant_sq * laplace_rows(extended)  43.4 us
    ppermute x8, starting transfers between devices, extended_2(): lax.ppermute(tail, axis, [(i, (i + 1) % count) for i in range(ends)])  42 us
    all_gather x1, waiting for transfers between devices, body(): shard_piece = lax.all_gather(fields, 'shot', axis=1, tiled=True)  30.6 us
    ppermute x8, waiting for transfers between devices, extended_2(): lax.ppermute(head, axis, [((i + 1) % count, i) for i in range(ends)])  16.2 us
    another operation x16, local copies, waits for them, and re-layouts  11.3 us
    select_n x8, other arithmetic, body(): updated = jnp.where(inside[None, None, :, None, None], updated, 0.0)  11.2 us
    ppermute x8, starting transfers between devices, extended_2(): lax.ppermute(head, axis, [((i + 1) % count, i) for i in range(ends)])  10.5 us
  transfers between devices with their start and end apart: 17, of which 17 were waited for; matrix products, arithmetic and copies ran while one was open for 2% of the time, Pallas kernels for 0%

commit v1 on v0

--- a/solution.py
+++ b/solution.py
@@ -103,7 +103,16 @@
     half_span = offset_perm.shape[0] // 2
     pad_widths = ((0, 0), (0, 0), (half_span, half_span), (0, 0))
     own_lags = lax.dynamic_slice_in_dim(offset_perm, lax.axis_index("shot") * OFF_DEV, OFF_DEV)
-    shard_piece = lax.all_gather(fields, "shot", axis=1, tiled=True)
+    ways = lax.axis_size("shot")
+    up = [(d, (d + 1) % ways) for d in range(ways)]
+    down = [(d, (d - 1) % ways) for d in range(ways)]
+    earlier, later = ([fields], [fields])
+    for _ in range(ways // 2):
+        earlier.append(lax.ppermute(earlier[-1], "shot", up))
+    for _ in range((ways - 1) // 2):
+        later.append(lax.ppermute(later[-1], "shot", down))
+    line = jnp.concatenate([*earlier[::-1], *later[1:]], axis=1)
+    shard_piece = jnp.roll(line, (lax.axis_index("shot") - ways // 2) * fields.shape[1], axis=1)
     source_pad = jnp.pad(shard_piece[0], pad_widths)
     receiver_pad = jnp.pad(shard_piece[1], pad_widths)
     products = [

time: 273 us -> 262 us (0.960)
  between operations: 19.9 us -> 6.62 us
    all_gather x1 -> x0, waiting for transfers between devices: 30.6 us -> none  [body(): shard_piece = lax.all_gather(fields, 'shot', axis=1, tiled=True)]
    ppermute x0 -> x3, waiting for transfers between devices: none -> 29.5 us  [the longest x2 29.5 us: body(): earlier.append(lax.ppermute(earlier[-1], 'shot', up))]
    unnamed x60 -> x63, local copies, waits for them, and re-layouts: 4.44 us -> 7.16 us
  transfers between devices with their start and end apart: 17 -> 19, of which waited for: 17 -> 18; matrix products, arithmetic and copies ran while one was open for 2% -> 4% of each run, Pallas kernels for 0% -> 0%
where the time goes in v1:
time: 262 us; the launch traced here: 260 us
  local copies, waits for them, and re-layouts  81.9 us (31%)
  other arithmetic  59.7 us (23%)
  waiting for transfers between devices  54.6 us (21%)
  starting transfers between devices  54.1 us (21%)
  between operations  6.62 us (3%)
    scatter-add x8, local copies, waits for them, and re-layouts, body(): updated = updated.at[:, :, :, :, INJECT_Z].add(planes)  53 us
    add x8, other arithmetic, body(): updated = 2.0 * centre - before + courant_sq * laplace_rows(extended)  43.4 us
    ppermute x8, starting transfers between devices, extended_2(): lax.ppermute(tail, axis, [(i, (i + 1) % count) for i in range(ends)])  42 us
    ppermute x2, waiting for transfers between devices, body(): earlier.append(lax.ppermute(earlier[-1], 'shot', up))  29.5 us
    ppermute x8, waiting for transfers between devices, extended_2(): lax.ppermute(head, axis, [((i + 1) % count, i) for i in range(ends)])  15 us
    another operation x16, local copies, waits for them, and re-layouts  11.3 us
    ppermute x8, starting transfers between devices, extended_2(): lax.ppermute(head, axis, [((i + 1) % count, i) for i in range(ends)])  10.3 us
    ppermute x8, waiting for transfers between devices, extended_2(): lax.ppermute(tail, axis, [(i, (i + 1) % count) for i in range(ends)])  10.2 us
  transfers between devices with their start and end apart: 19, of which 18 were waited for; matrix products, arithmetic and copies ran while one was open for 4% of the time, Pallas kernels for 0%

profile of v1, /device:TPU:0, one launch (start us, length us, event | category | flops | bytes accessed | tf_op | source)
XLA Modules:
  0.0 259.7 jit_solution(9029449336668220096)
XLA Ops:
  3.2 5.6 %collective-permute-start.1 = (f32[2,2,4,16,256]{4,3,2,1,0:T(8,128)S(1)}, f32[2,2,4,16,256]{4,3,2,1,0:T(8,128)S(1)}, u32[]{:S(2)}, u32[]{:S(2)}) collective-permute-start(f32[2,2,4,16,256]{4,3,2,1,0:T(8,128)S(1)} %get-tuple-element.139), channel_id=1, source_target_pairs={{0,1},{1,2},{2,3},{4,5},{5,6},{6,7},{8,9},{9,10},{10,11},{12,13},{... | collective-permute-start | bytes 786440 | tf_op jit(solution)/shard_map/ppermute | solution.py:21
  19.1 5.4 %scatter-add.26 = f32[2,2,16,16,256]{4,3,2,1,0:T(8,128)S(1)} dynamic-update-slice(f32[2,2,16,16,256]{4,3,2,1,0:T(8,128)S(1)} %fusion.216, f32[2,2,16,16,1]{4,3,2,1,0:T(8,128)S(1)} %copy.253, s32[]{:T(128)} %constant.233.clone.1, s32[]{:T(128)} %constant.233.clone.1, s32[]{:T(128)} %constant.233.clone.1, s32[]{:T(128)} %constant.233.clone.1, s32[]{:T(128)} %constant.247.clone.1) | dynamic-update-slice | bytes 8196 | tf_op jit(solution)/shard_map/scatter-add | solution.py:98
  26.9 5.7 %collective-permute-start.3 = (f32[2,2,4,16,256]{4,3,2,1,0:T(8,128)S(1)}, f32[2,2,4,16,256]{4,3,2,1,0:T(8,128)}, u32[]{:S(2)}, u32[]{:S(2)}) collective-permute-start(f32[2,2,4,16,256]{4,3,2,1,0:T(8,128)S(1)} %get-tuple-element.135), channel_id=1, source_target_pairs={{0,1},{1,2},{2,3},{4,5},{5,6},{6,7},{8,9},{9,10},{10,11},{12,13},{... | collective-permute-start | bytes 786440 | tf_op jit(solution)/shard_map/ppermute | solution.py:21
  36.6 14.1 %fusion.186 = f32[2,2,16,16,256]{4,3,2,1,0:T(8,128)S(1)} fusion(f32[2,2,16,16,256]{4,3,2,1,0:T(8,128)} %copy-done.10, f32[2,2,4,16,256]{4,3,2,1,0:T(8,128)} %collective-permute-done.3, f32[2,2,4,16,256]{4,3,2,1,0:T(8,128)} %copy-done.13, f32[16,16,256]{2,1,0:T(8,128)S(1)} %copy-done.1, f32[1,2,16,16,256]{4,3,2,1,0:T(8,128)S(1)} %bitcast.77, ...), kind=kLoop, calls=%fused_computation.411 | loop fusion | flops 13107200 | bytes 3932160 | tf_op jit(solution)/shard_map/add | solution.py:89
  51.9 6.8 %scatter-add.29 = f32[2,2,16,16,256]{4,3,2,1,0:T(8,128)} dynamic-update-slice(f32[2,2,16,16,256]{4,3,2,1,0:T(8,128)} %copy-done.6, f32[2,2,16,16,1]{4,3,2,1,0:T(8,128)S(1)} %copy.256, s32[]{:T(128)} %constant.233.clone.1, s32[]{:T(128)} %constant.233.clone.1, s32[]{:T(128)} %constant.233.clone.1, s32[]{:T(128)} %constant.233.clone.1, s32[]{:T(128)} %constant.247.clone.1) | dynamic-update-slice | bytes 8196 | tf_op jit(solution)/shard_map/scatter-add | solution.py:98
  61.3 5.1 %collective-permute-start.5 = (f32[2,2,4,16,256]{4,3,2,1,0:T(8,128)S(1)}, f32[2,2,4,16,256]{4,3,2,1,0:T(8,128)S(1)}, u32[]{:S(2)}, u32[]{:S(2)}) collective-permute-start(f32[2,2,4,16,256]{4,3,2,1,0:T(8,128)S(1)} %get-tuple-element.133), channel_id=1, source_target_pairs={{0,1},{1,2},{2,3},{4,5},{5,6},{6,7},{8,9},{9,10},{10,11},{12,13},{... | collective-permute-start | bytes 786440 | tf_op jit(solution)/shard_map/ppermute | solution.py:21
  70.3 4.5 %fusion.160 = f32[2,2,16,16,256]{4,3,2,1,0:T(8,128)} fusion(f32[2,2,16,16,256]{4,3,2,1,0:T(8,128)S(1)} %broadcast_select_fusion.6, f32[2,2,4,16,256]{4,3,2,1,0:T(8,128)S(1)} %collective-permute-done.5, f32[2,2,4,16,256]{4,3,2,1,0:T(8,128)S(1)} %collective-permute-done.4, f32[16,16,256]{2,1,0:T(8,128)S(1)} %copy-done.1, ...), kind=kLoop, calls=%fused_computation.385 | loop fusion | flops 13107200 | bytes 3932176 | tf_op jit(solution)/shard_map/add | solution.py:89
  77.0 6.8 %scatter-add.30 = f32[2,2,16,16,256]{4,3,2,1,0:T(8,128)} dynamic-update-slice(f32[2,2,16,16,256]{4,3,2,1,0:T(8,128)} %fusion.160, f32[2,2,16,16,1]{4,3,2,1,0:T(8,128)S(1)} %copy.259, s32[]{:T(128)} %constant.233.clone.1, s32[]{:T(128)} %constant.233.clone.1, s32[]{:T(128)} %constant.233.clone.1, s32[]{:T(128)} %constant.233.clone.1, s32[]{:T(128)} %constant.247.clone.1) | dynamic-update-slice | bytes 8196 | tf_op jit(solution)/shard_map/scatter-add | solution.py:98
  86.5 5.2 %collective-permute-start.7 = (f32[2,2,4,16,256]{4,3,2,1,0:T(8,128)S(1)}, f32[2,2,4,16,256]{4,3,2,1,0:T(8,128)S(1)}, u32[]{:S(2)}, u32[]{:S(2)}) collective-permute-start(f32[2,2,4,16,256]{4,3,2,1,0:T(8,128)S(1)} %get-tuple-element.131), channel_id=1, source_target_pairs={{0,1},{1,2},{2,3},{4,5},{5,6},{6,7},{8,9},{9,10},{10,11},{12,13},{... | collective-permute-start | bytes 786440 | tf_op jit(solution)/shard_map/ppermute | solution.py:21
  102.0 6.8 %scatter-add.31 = f32[2,2,16,16,256]{4,3,2,1,0:T(8,128)} dynamic-update-slice(f32[2,2,16,16,256]{4,3,2,1,0:T(8,128)} %fusion.134, f32[2,2,16,16,1]{4,3,2,1,0:T(8,128)S(1)} %copy.262, s32[]{:T(128)} %constant.233.clone.1, s32[]{:T(128)} %constant.233.clone.1, s32[]{:T(128)} %constant.233.clone.1, s32[]{:T(128)} %constant.233.clone.1, s32[]{:T(128)} %constant.247.clone.1) | dynamic-update-slice | bytes 8196 | tf_op jit(solution)/shard_map/scatter-add | solution.py:98
  111.6 5.0 %collective-permute-start.9 = (f32[2,2,4,16,256]{4,3,2,1,0:T(8,128)S(1)}, f32[2,2,4,16,256]{4,3,2,1,0:T(8,128)S(1)}, u32[]{:S(2)}, u32[]{:S(2)}) collective-permute-start(f32[2,2,4,16,256]{4,3,2,1,0:T(8,128)S(1)} %get-tuple-element.129), channel_id=1, source_target_pairs={{0,1},{1,2},{2,3},{4,5},{5,6},{6,7},{8,9},{9,10},{10,11},{12,13},{... | collective-permute-start | bytes 786440 | tf_op jit(solution)/shard_map/ppermute | solution.py:21
  120.5 4.5 %fusion.108 = f32[2,2,16,16,256]{4,3,2,1,0:T(8,128)} fusion(f32[2,2,16,16,256]{4,3,2,1,0:T(8,128)S(1)} %broadcast_select_fusion.4, f32[2,2,4,16,256]{4,3,2,1,0:T(8,128)S(1)} %collective-permute-done.9, f32[2,2,4,16,256]{4,3,2,1,0:T(8,128)S(1)} %collective-permute-done.8, f32[16,16,256]{2,1,0:T(8,128)S(1)} %copy-done.1, ...), kind=kLoop, calls=%fused_computation.333 | loop fusion | flops 13107200 | bytes 3932176 | tf_op jit(solution)/shard_map/add | solution.py:89
  127.1 6.8 %scatter-add.34 = f32[2,2,16,16,256]{4,3,2,1,0:T(8,128)} dynamic-update-slice(f32[2,2,16,16,256]{4,3,2,1,0:T(8,128)} %fusion.108, f32[2,2,16,16,1]{4,3,2,1,0:T(8,128)S(1)} %copy.265, s32[]{:T(128)} %constant.233.clone.1, s32[]{:T(128)} %constant.233.clone.1, s32[]{:T(128)} %constant.233.clone.1, s32[]{:T(128)} %constant.233.clone.1, s32[]{:T(128)} %constant.247.clone.1) | dynamic-update-slice | bytes 8196 | tf_op jit(solution)/shard_map/scatter-add | solution.py:98
  136.7 5.0 %collective-permute-start.11 = (f32[2,2,4,16,256]{4,3,2,1,0:T(8,128)S(1)}, f32[2,2,4,16,256]{4,3,2,1,0:T(8,128)S(1)}, u32[]{:S(2)}, u32[]{:S(2)}) collective-permute-start(f32[2,2,4,16,256]{4,3,2,1,0:T(8,128)S(1)} %get-tuple-element.127), channel_id=1, source_target_pairs={{0,1},{1,2},{2,3},{4,5},{5,6},{6,7},{8,9},{9,10},{10,11},{12,13},{... | collective-permute-start | bytes 786440 | tf_op jit(solution)/shard_map/ppermute | solution.py:21
  145.6 4.5 %fusion.82 = f32[2,2,16,16,256]{4,3,2,1,0:T(8,128)} fusion(f32[2,2,16,16,256]{4,3,2,1,0:T(8,128)S(1)} %broadcast_select_fusion.3, f32[2,2,4,16,256]{4,3,2,1,0:T(8,128)S(1)} %collective-permute-done.11, f32[2,2,4,16,256]{4,3,2,1,0:T(8,128)S(1)} %collective-permute-done.10, f32[16,16,256]{2,1,0:T(8,128)S(1)} %copy-done.1, ...), kind=kLoop, calls=%fused_computation.307 | loop fusion | flops 13107200 | bytes 3932176 | tf_op jit(solution)/shard_map/add | solution.py:89
  152.2 6.8 %scatter-add.35 = f32[2,2,16,16,256]{4,3,2,1,0:T(8,128)} dynamic-update-slice(f32[2,2,16,16,256]{4,3,2,1,0:T(8,128)} %fusion.82, f32[2,2,16,16,1]{4,3,2,1,0:T(8,128)S(1)} %copy.268, s32[]{:T(128)} %constant.233.clone.1, s32[]{:T(128)} %constant.233.clone.1, s32[]{:T(128)} %constant.233.clone.1, s32[]{:T(128)} %constant.233.clone.1, s32[]{:T(128)} %constant.247.clone.1) | dynamic-update-slice | bytes 8196 | tf_op jit(solution)/shard_map/scatter-add | solution.py:98
  161.7 5.3 %collective-permute-start.13 = (f32[2,2,4,16,256]{4,3,2,1,0:T(8,128)S(1)}, f32[2,2,4,16,256]{4,3,2,1,0:T(8,128)S(1)}, u32[]{:S(2)}, u32[]{:S(2)}) collective-permute-start(f32[2,2,4,16,256]{4,3,2,1,0:T(8,128)S(1)} %get-tuple-element.125), channel_id=1, source_target_pairs={{0,1},{1,2},{2,3},{4,5},{5,6},{6,7},{8,9},{9,10},{10,11},{12,13},{... | collective-permute-start | bytes 786440 | tf_op jit(solution)/shard_map/ppermute | solution.py:21
  170.6 4.5 %fusion.56 = f32[2,2,16,16,256]{4,3,2,1,0:T(8,128)} fusion(f32[2,2,16,16,256]{4,3,2,1,0:T(8,128)S(1)} %broadcast_select_fusion.2, f32[2,2,4,16,256]{4,3,2,1,0:T(8,128)S(1)} %collective-permute-done.13, f32[2,2,4,16,256]{4,3,2,1,0:T(8,128)S(1)} %collective-permute-done.12, f32[16,16,256]{2,1,0:T(8,128)S(1)} %copy-done.1, ...), kind=kLoop, calls=%fused_computation.281 | loop fusion | flops 13107200 | bytes 3932176 | tf_op jit(solution)/shard_map/add | solution.py:89
  177.3 6.8 %scatter-add.36 = f32[2,2,16,16,256]{4,3,2,1,0:T(8,128)} dynamic-update-slice(f32[2,2,16,16,256]{4,3,2,1,0:T(8,128)} %fusion.56, f32[2,2,16,16,1]{4,3,2,1,0:T(8,128)S(1)} %copy.271, s32[]{:T(128)} %constant.233.clone.1, s32[]{:T(128)} %constant.233.clone.1, s32[]{:T(128)} %constant.233.clone.1, s32[]{:T(128)} %constant.233.clone.1, s32[]{:T(128)} %constant.247.clone.1) | dynamic-update-slice | bytes 8196 | tf_op jit(solution)/shard_map/scatter-add | solution.py:98
  186.8 5.0 %collective-permute-start.15 = (f32[2,2,4,16,256]{4,3,2,1,0:T(8,128)S(1)}, f32[2,2,4,16,256]{4,3,2,1,0:T(8,128)S(1)}, u32[]{:S(2)}, u32[]{:S(2)}) collective-permute-start(f32[2,2,4,16,256]{4,3,2,1,0:T(8,128)S(1)} %get-tuple-element.123), channel_id=1, source_target_pairs={{0,1},{1,2},{2,3},{4,5},{5,6},{6,7},{8,9},{9,10},{10,11},{12,13},{... | collective-permute-start | bytes 786440 | tf_op jit(solution)/shard_map/ppermute | solution.py:21
  195.7 4.5 %fusion.30 = f32[2,2,16,16,256]{4,3,2,1,0:T(8,128)} fusion(f32[2,2,16,16,256]{4,3,2,1,0:T(8,128)S(1)} %broadcast_select_fusion.1, f32[2,2,4,16,256]{4,3,2,1,0:T(8,128)S(1)} %collective-permute-done.15, f32[2,2,4,16,256]{4,3,2,1,0:T(8,128)S(1)} %collective-permute-done.14, f32[16,16,256]{2,1,0:T(8,128)S(1)} %copy-done.1, ...), kind=kLoop, calls=%fused_computation.255 | loop fusion | flops 13107200 | bytes 3932176 | tf_op jit(solution)/shard_map/add | solution.py:89
  202.3 6.7 %scatter-add.39 = f32[2,2,16,16,256]{4,3,2,1,0:T(8,128)} dynamic-update-slice(f32[2,2,16,16,256]{4,3,2,1,0:T(8,128)} %fusion.30, f32[2,2,16,16,1]{4,3,2,1,0:T(8,128)S(1)} %copy.274, s32[]{:T(128)} %constant.233.clone.1, s32[]{:T(128)} %constant.233.clone.1, s32[]{:T(128)} %constant.233.clone.1, s32[]{:T(128)} %constant.233.clone.1, s32[]{:T(128)} %constant.247.clone.1) | dynamic-update-slice | bytes 8196 | tf_op jit(solution)/shard_map/scatter-add | solution.py:98
  210.5 14.2 %collective-permute-done.16 = f32[2,2,16,16,256]{4,3,2,1,0:T(8,128)S(1)} collective-permute-done((f32[2,2,16,16,256]{4,3,2,1,0:T(8,128)S(1)}, f32[2,2,16,16,256]{4,3,2,1,0:T(8,128)S(1)}, u32[]{:S(2)}, u32[]{:S(2)}) %collective-permute-start.16) | collective-permute-done | bytes 1048608 | tf_op jit(solution)/shard_map/ppermute | solution.py:111
  233.4 15.2 %collective-permute-done.17 = f32[2,2,16,16,256]{4,3,2,1,0:T(8,128)} collective-permute-done((f32[2,2,16,16,256]{4,3,2,1,0:T(8,128)S(1)}, f32[2,2,16,16,256]{4,3,2,1,0:T(8,128)}, u32[]{:S(2)}, u32[]{:S(2)}) %collective-permute-start.17) | collective-permute-done | bytes 1048608 | tf_op jit(solution)/shard_map/ppermute | solution.py:111
  (184 shorter events, 92.1 us)
Async XLA Ops:
  1.9 11.3 %collective-permute-start = (f32[2,2,4,16,256]{4,3,2,1,0:T(8,128)S(1)}, f32[2,2,4,16,256]{4,3,2,1,0:T(8,128)S(1)}, u32[]{:S(2)}, u32[]{:S(2)}) collective-permute-start(f32[2,2,4,16,256]{4,3,2,1,0:T(8,128)S(1)} %get-tuple-element.138), channel_id=1, source_target_pairs={{1,0},{2,1},{3,2},{5,4},{6,5},{7,6},{9,8},{10,9},{11,10},{13,12},{... | collective-permute-start | bytes 786440 | tf_op jit(solution)/shard_map/ppermute | solution.py:23
  3.2 11.1 %collective-permute-start.1 = (f32[2,2,4,16,256]{4,3,2,1,0:T(8,128)S(1)}, f32[2,2,4,16,256]{4,3,2,1,0:T(8,128)S(1)}, u32[]{:S(2)}, u32[]{:S(2)}) collective-permute-start(f32[2,2,4,16,256]{4,3,2,1,0:T(8,128)S(1)} %get-tuple-element.139), channel_id=1, source_target_pairs={{0,1},{1,2},{2,3},{4,5},{5,6},{6,7},{8,9},{9,10},{10,11},{12,13},{... | collective-permute-start | bytes 786440 | tf_op jit(solution)/shard_map/ppermute | solution.py:21
  25.6 9.8 %collective-permute-start.2 = (f32[2,2,4,16,256]{4,3,2,1,0:T(8,128)S(1)}, f32[2,2,4,16,256]{4,3,2,1,0:T(8,128)S(1)}, u32[]{:S(2)}, u32[]{:S(2)}) collective-permute-start(f32[2,2,4,16,256]{4,3,2,1,0:T(8,128)S(1)} %get-tuple-element.134), channel_id=1, source_target_pairs={{1,0},{2,1},{3,2},{5,4},{6,5},{7,6},{9,8},{10,9},{11,10},{13,12},{... | collective-permute-start | bytes 786440 | tf_op jit(solution)/shard_map/ppermute | solution.py:23
  26.9 9.7 %collective-permute-start.3 = (f32[2,2,4,16,256]{4,3,2,1,0:T(8,128)S(1)}, f32[2,2,4,16,256]{4,3,2,1,0:T(8,128)}, u32[]{:S(2)}, u32[]{:S(2)}) collective-permute-start(f32[2,2,4,16,256]{4,3,2,1,0:T(8,128)S(1)} %get-tuple-element.135), channel_id=1, source_target_pairs={{0,1},{1,2},{2,3},{4,5},{5,6},{6,7},{8,9},{9,10},{10,11},{12,13},{... | collective-permute-start | bytes 786440 | tf_op jit(solution)/shard_map/ppermute | solution.py:21
  60.0 9.1 %collective-permute-start.4 = (f32[2,2,4,16,256]{4,3,2,1,0:T(8,128)S(1)}, f32[2,2,4,16,256]{4,3,2,1,0:T(8,128)S(1)}, u32[]{:S(2)}, u32[]{:S(2)}) collective-permute-start(f32[2,2,4,16,256]{4,3,2,1,0:T(8,128)S(1)} %get-tuple-element.132), channel_id=1, source_target_pairs={{1,0},{2,1},{3,2},{5,4},{6,5},{7,6},{9,8},{10,9},{11,10},{13,12},{... | collective-permute-start | bytes 786440 | tf_op jit(solution)/shard_map/ppermute | solution.py:23
  61.3 9.0 %collective-permute-start.5 = (f32[2,2,4,16,256]{4,3,2,1,0:T(8,128)S(1)}, f32[2,2,4,16,256]{4,3,2,1,0:T(8,128)S(1)}, u32[]{:S(2)}, u32[]{:S(2)}) collective-permute-start(f32[2,2,4,16,256]{4,3,2,1,0:T(8,128)S(1)} %get-tuple-element.133), channel_id=1, source_target_pairs={{0,1},{1,2},{2,3},{4,5},{5,6},{6,7},{8,9},{9,10},{10,11},{12,13},{... | collective-permute-start | bytes 786440 | tf_op jit(solution)/shard_map/ppermute | solution.py:21
  77.0 18.4 %copy-start.7 = (f32[2,2,16,16,256]{4,3,2,1,0:T(8,128)S(1)}, f32[2,2,16,16,256]{4,3,2,1,0:T(8,128)}, u32[]{:S(2)}) copy-start(f32[2,2,16,16,256]{4,3,2,1,0:T(8,128)} %scatter-add.29) | copy-start | bytes 3145732
  85.2 8.7 %collective-permute-start.6 = (f32[2,2,4,16,256]{4,3,2,1,0:T(8,128)S(1)}, f32[2,2,4,16,256]{4,3,2,1,0:T(8,128)S(1)}, u32[]{:S(2)}, u32[]{:S(2)}) collective-permute-start(f32[2,2,4,16,256]{4,3,2,1,0:T(8,128)S(1)} %get-tuple-element.130), channel_id=1, source_target_pairs={{1,0},{2,1},{3,2},{5,4},{6,5},{7,6},{9,8},{10,9},{11,10},{13,12},{... | collective-permute-start | bytes 786440 | tf_op jit(solution)/shard_map/ppermute | solution.py:23
  86.5 8.9 %collective-permute-start.7 = (f32[2,2,4,16,256]{4,3,2,1,0:T(8,128)S(1)}, f32[2,2,4,16,256]{4,3,2,1,0:T(8,128)S(1)}, u32[]{:S(2)}, u32[]{:S(2)}) collective-permute-start(f32[2,2,4,16,256]{4,3,2,1,0:T(8,128)S(1)} %get-tuple-element.131), channel_id=1, source_target_pairs={{0,1},{1,2},{2,3},{4,5},{5,6},{6,7},{8,9},{9,10},{10,11},{12,13},{... | collective-permute-start | bytes 786440 | tf_op jit(solution)/shard_map/ppermute | solution.py:21
  102.0 18.5 %copy-start.2 = (f32[2,2,16,16,256]{4,3,2,1,0:T(8,128)S(1)}, f32[2,2,16,16,256]{4,3,2,1,0:T(8,128)}, u32[]{:S(2)}) copy-start(f32[2,2,16,16,256]{4,3,2,1,0:T(8,128)} %scatter-add.30) | copy-start | bytes 3145732
  110.3 8.7 %collective-permute-start.8 = (f32[2,2,4,16,256]{4,3,2,1,0:T(8,128)S(1)}, f32[2,2,4,16,256]{4,3,2,1,0:T(8,128)S(1)}, u32[]{:S(2)}, u32[]{:S(2)}) collective-permute-start(f32[2,2,4,16,256]{4,3,2,1,0:T(8,128)S(1)} %get-tuple-element.128), channel_id=1, source_target_pairs={{1,0},{2,1},{3,2},{5,4},{6,5},{7,6},{9,8},{10,9},{11,10},{13,12},{... | collective-permute-start | bytes 786440 | tf_op jit(solution)/shard_map/ppermute | solution.py:23
  111.6 8.9 %collective-permute-start.9 = (f32[2,2,4,16,256]{4,3,2,1,0:T(8,128)S(1)}, f32[2,2,4,16,256]{4,3,2,1,0:T(8,128)S(1)}, u32[]{:S(2)}, u32[]{:S(2)}) collective-permute-start(f32[2,2,4,16,256]{4,3,2,1,0:T(8,128)S(1)} %get-tuple-element.129), channel_id=1, source_target_pairs={{0,1},{1,2},{2,3},{4,5},{5,6},{6,7},{8,9},{9,10},{10,11},{12,13},{... | collective-permute-start | bytes 786440 | tf_op jit(solution)/shard_map/ppermute | solution.py:21
  127.1 18.4 %copy-start.3 = (f32[2,2,16,16,256]{4,3,2,1,0:T(8,128)S(1)}, f32[2,2,16,16,256]{4,3,2,1,0:T(8,128)}, u32[]{:S(2)}) copy-start(f32[2,2,16,16,256]{4,3,2,1,0:T(8,128)} %scatter-add.31) | copy-start | bytes 3145732
  135.4 8.7 %collective-permute-start.10 = (f32[2,2,4,16,256]{4,3,2,1,0:T(8,128)S(1)}, f32[2,2,4,16,256]{4,3,2,1,0:T(8,128)S(1)}, u32[]{:S(2)}, u32[]{:S(2)}) collective-permute-start(f32[2,2,4,16,256]{4,3,2,1,0:T(8,128)S(1)} %get-tuple-element.126), channel_id=1, source_target_pairs={{1,0},{2,1},{3,2},{5,4},{6,5},{7,6},{9,8},{10,9},{11,10},{13,12},{... | collective-permute-start | bytes 786440 | tf_op jit(solution)/shard_map/ppermute | solution.py:23
  136.7 8.9 %collective-permute-start.11 = (f32[2,2,4,16,256]{4,3,2,1,0:T(8,128)S(1)}, f32[2,2,4,16,256]{4,3,2,1,0:T(8,128)S(1)}, u32[]{:S(2)}, u32[]{:S(2)}) collective-permute-start(f32[2,2,4,16,256]{4,3,2,1,0:T(8,128)S(1)} %get-tuple-element.127), channel_id=1, source_target_pairs={{0,1},{1,2},{2,3},{4,5},{5,6},{6,7},{8,9},{9,10},{10,11},{12,13},{... | collective-permute-start | bytes 786440 | tf_op jit(solution)/shard_map/ppermute | solution.py:21
  152.2 18.5 %copy-start.4 = (f32[2,2,16,16,256]{4,3,2,1,0:T(8,128)S(1)}, f32[2,2,16,16,256]{4,3,2,1,0:T(8,128)}, u32[]{:S(2)}) copy-start(f32[2,2,16,16,256]{4,3,2,1,0:T(8,128)} %scatter-add.34) | copy-start | bytes 3145732
  160.4 8.7 %collective-permute-start.12 = (f32[2,2,4,16,256]{4,3,2,1,0:T(8,128)S(1)}, f32[2,2,4,16,256]{4,3,2,1,0:T(8,128)S(1)}, u32[]{:S(2)}, u32[]{:S(2)}) collective-permute-start(f32[2,2,4,16,256]{4,3,2,1,0:T(8,128)S(1)} %get-tuple-element.124), channel_id=1, source_target_pairs={{1,0},{2,1},{3,2},{5,4},{6,5},{7,6},{9,8},{10,9},{11,10},{13,12},{... | collective-permute-start | bytes 786440 | tf_op jit(solution)/shard_map/ppermute | solution.py:23
  161.7 8.9 %collective-permute-start.13 = (f32[2,2,4,16,256]{4,3,2,1,0:T(8,128)S(1)}, f32[2,2,4,16,256]{4,3,2,1,0:T(8,128)S(1)}, u32[]{:S(2)}, u32[]{:S(2)}) collective-permute-start(f32[2,2,4,16,256]{4,3,2,1,0:T(8,128)S(1)} %get-tuple-element.125), channel_id=1, source_target_pairs={{0,1},{1,2},{2,3},{4,5},{5,6},{6,7},{8,9},{9,10},{10,11},{12,13},{... | collective-permute-start | bytes 786440 | tf_op jit(solution)/shard_map/ppermute | solution.py:21
  185.5 8.7 %collective-permute-start.14 = (f32[2,2,4,16,256]{4,3,2,1,0:T(8,128)S(1)}, f32[2,2,4,16,256]{4,3,2,1,0:T(8,128)S(1)}, u32[]{:S(2)}, u32[]{:S(2)}) collective-permute-start(f32[2,2,4,16,256]{4,3,2,1,0:T(8,128)S(1)} %get-tuple-element.122), channel_id=1, source_target_pairs={{1,0},{2,1},{3,2},{5,4},{6,5},{7,6},{9,8},{10,9},{11,10},{13,12},{... | collective-permute-start | bytes 786440 | tf_op jit(solution)/shard_map/ppermute | solution.py:23
  186.8 8.9 %collective-permute-start.15 = (f32[2,2,4,16,256]{4,3,2,1,0:T(8,128)S(1)}, f32[2,2,4,16,256]{4,3,2,1,0:T(8,128)S(1)}, u32[]{:S(2)}, u32[]{:S(2)}) collective-permute-start(f32[2,2,4,16,256]{4,3,2,1,0:T(8,128)S(1)} %get-tuple-element.123), channel_id=1, source_target_pairs={{0,1},{1,2},{2,3},{4,5},{5,6},{6,7},{8,9},{9,10},{10,11},{12,13},{... | collective-permute-start | bytes 786440 | tf_op jit(solution)/shard_map/ppermute | solution.py:21
  201.4 25.1 %copy-start.24 = (s32[8]{0:T(128)S(1)}, s32[8]{0:T(128)}, u32[]{:S(2)}) copy-start(s32[8]{0:T(128)} %param.35) | copy-start | bytes 100
  210.4 14.3 %collective-permute-start.16 = (f32[2,2,16,16,256]{4,3,2,1,0:T(8,128)S(1)}, f32[2,2,16,16,256]{4,3,2,1,0:T(8,128)S(1)}, u32[]{:S(2)}, u32[]{:S(2)}) collective-permute-start(f32[2,2,16,16,256]{4,3,2,1,0:T(8,128)S(1)} %broadcast_select_fusion), channel_id=1, source_target_pairs={{0,4},{4,8},{8,12},{12,0},{1,5},{5,9},{9,13},{13,1},{2,6},{6,10},{... | collective-permute-start | bytes 3145736 | tf_op jit(solution)/shard_map/ppermute | solution.py:111
  224.7 23.9 %collective-permute-start.17 = (f32[2,2,16,16,256]{4,3,2,1,0:T(8,128)S(1)}, f32[2,2,16,16,256]{4,3,2,1,0:T(8,128)}, u32[]{:S(2)}, u32[]{:S(2)}) collective-permute-start(f32[2,2,16,16,256]{4,3,2,1,0:T(8,128)S(1)} %collective-permute-done.16), channel_id=1, source_target_pairs={{0,4},{4,8},{8,12},{12,0},{1,5},{5,9},{9,13},{13,1},{2,6},{6,10},{... | collective-permute-start | bytes 3145736 | tf_op jit(solution)/shard_map/ppermute | solution.py:111
  224.7 25.4 %collective-permute-start.18 = (f32[2,2,16,16,256]{4,3,2,1,0:T(8,128)S(1)}, f32[2,2,16,16,256]{4,3,2,1,0:T(8,128)S(1)}, u32[]{:S(2)}, u32[]{:S(2)}) collective-permute-start(f32[2,2,16,16,256]{4,3,2,1,0:T(8,128)S(1)} %broadcast_select_fusion), channel_id=1, source_target_pairs={{0,12},{4,0},{8,4},{12,8},{1,13},{5,1},{9,5},{13,9},{2,14},{6,2},{... | collective-permute-start | bytes 3145736 | tf_op jit(solution)/shard_map/ppermute | solution.py:113
  (23 other events, 229.2 us)
